TPU v7x, 256 devices: a whole 4x4x8 slice. The times are simulated.
256 devices in a mesh: mem: 16 (over y_lo, z), lat: 4 (over x), lon: 4 (over y_hi, core).
Axes of the slice: x: 4, y: 4 (y_hi: 2, y_lo: 2; y = y_hi * 2 + y_lo), z: 8, core: 2. Of those that a mesh axis runs over, the one named last changes fastest.
Arguments:
- ensemble: bfloat16 [256, 73, 32, 512], P('mem', None, 'lat', 'lon'), may hold values from -6 to 6
- ancestry: int32 [256], replicated, may hold values from 0 to 255, as said below
- obs_weights: float32 [256], P('mem'), may hold values from 0.1 to 10
- kernel_index: int32 [32], P('lat'), may hold values from 0 to 7
- kernel_table: float32 [8, 9, 73], replicated, may hold values from -3 to 3
- feature_scaling_factor: float32 [73], replicated, may hold values from 0.1 to 1.9
- entry_projection_matrix: bfloat16 [1536, 73], replicated, may hold values from -0.75 to 0.75
- exit_projection_matrix: bfloat16 [73, 1536], replicated, may hold values from -0.15625 to 0.15625
Outputs:
- predicted_particles: bfloat16 [256, 73, 32, 512], P('mem', None, 'lat', 'lon')
- importance_average_state: float32 [73, 32, 512], P(None, 'lat', 'lon')
Inputs may be any that keep to these rules, and one draw needn't show every extreme that they name: `ancestry`: each slot's ancestor member. The slots held by one index of mem take at most 1 distinct ancestors from the members held by any one index of mem.
All inputs are finite; a program needn't handle non-finite values.
Results may differ from a plain program's by a relative error of at most 0.0042.
Values may be sent and summed in bfloat16 or wider, within the bound.
No kernel may reach another device: no remote copies, remote signals or barrier semaphores. Data moves between devices by JAX's collectives and lax.ppermute only.
A program may use at most 128 MiB of HBM per device.

v0:
```python
import jax
import jax.numpy as jnp
from jax import lax
from jax.sharding import PartitionSpec as P

EPS = 1e-06


def extended(block, sides, width, periodic):
    for axis, dim in sides:
        count = lax.axis_size(axis)
        forward = [(i, i + 1) for i in range(count - 1)]
        if periodic:
            forward.append((count - 1, 0))
        backward = [(target, source) for source, target in forward]
        low = lax.ppermute(
            lax.slice_in_dim(block, block.shape[dim] - width, None, axis=dim), axis, forward
        )
        high = lax.ppermute(lax.slice_in_dim(block, 0, width, axis=dim), axis, backward)
        block = jnp.concatenate([low, block, high], axis=dim)
    return block


def finish(conv, field, feature_scaling_factor, entry_projection_matrix, exit_projection_matrix):
    mean_sq = jnp.mean(conv * conv, axis=0)
    normed = (conv * lax.rsqrt(mean_sq + EPS) * feature_scaling_factor[:, None, None]).astype(
        jnp.bfloat16
    )
    flat = normed.reshape(normed.shape[0], -1)
    hidden = jax.nn.gelu(
        jnp.dot(entry_projection_matrix, flat, preferred_element_type=jnp.float32), approximate=True
    ).astype(jnp.bfloat16)
    update = jnp.dot(
        exit_projection_matrix, hidden, preferred_element_type=jnp.float32
    ) + field.reshape(field.shape[0], -1)
    return update.reshape(field.shape).astype(jnp.bfloat16)


def propagate_particles(
    member_tiles,
    filter_coefficients,
    feature_scaling_factor,
    entry_projection_matrix,
    exit_projection_matrix,
):
    widened = extended(member_tiles, (("lat", 2),), 1, False)
    widened = extended(widened, (("lon", 3),), 1, True)

    def one_member(pair):
        particle_state, padded_tile = pair
        field = particle_state.astype(jnp.float32)
        padded = padded_tile.astype(jnp.float32)
        row_count = field.shape[1]
        col_count = field.shape[2]
        conv = jnp.zeros_like(field)
        for tap_index in range(9):
            row_shift = tap_index // 3
            col_shift = tap_index % 3
            conv = (
                conv
                + filter_coefficients[tap_index][:, :, None]
                * padded[:, row_shift : row_shift + row_count, col_shift : col_shift + col_count]
            )
        return finish(
            conv, field, feature_scaling_factor, entry_projection_matrix, exit_projection_matrix
        )

    return lax.map(one_member, (member_tiles, widened))


def replicate_tiles(member_tiles, ancestry):
    my_index = lax.axis_index("mem")
    per_device = member_tiles.shape[0]
    own_parents = lax.dynamic_slice_in_dim(ancestry, my_index * per_device, per_device)
    shard_rows = lax.all_gather(member_tiles, "mem", axis=0, tiled=True)
    row_total = shard_rows.shape[0]
    inside = (own_parents >= 0) & (own_parents < row_total)
    picked = jnp.take(shard_rows, jnp.clip(own_parents, 0, row_total - 1), axis=0)
    return jnp.where(inside[:, None, None, None], picked, jnp.zeros_like(member_tiles))


def shards(
    ensemble,
    ancestry,
    obs_weights,
    kernel_index,
    kernel_table,
    feature_scaling_factor,
    entry_projection_matrix,
    exit_projection_matrix,
):
    kernels = kernel_table.shape[0]
    onehot = (kernel_index[:, None] == jnp.arange(kernels, dtype=jnp.int32)[None, :]).astype(
        jnp.float32
    )
    flat_table = kernel_table.reshape(kernels, -1)
    filter_coefficients = jnp.dot(onehot, flat_table, precision=lax.Precision.HIGHEST)
    filter_coefficients = jnp.transpose(
        filter_coefficients.reshape(kernel_index.shape[0], 9, -1), (1, 2, 0)
    )
    predicted_particles = propagate_particles(
        replicate_tiles(ensemble, ancestry),
        filter_coefficients,
        feature_scaling_factor,
        entry_projection_matrix,
        exit_projection_matrix,
    )

    def accumulate(total, pair):
        weight, particle_state = pair
        return (total + weight * particle_state.astype(jnp.float32), None)

    start_total = jnp.zeros(ensemble.shape[1:], jnp.float32)
    weighted_part, _ = lax.scan(accumulate, start_total, (obs_weights, ensemble))
    importance_aggregate, likelihood_normalizer = lax.psum(
        (weighted_part, jnp.sum(obs_weights)), "mem"
    )
    return (predicted_particles, importance_aggregate / likelihood_normalizer)


def solution(mesh):
    return jax.shard_map(
        shards,
        mesh=mesh,
        in_specs=(P("mem", None, "lat", "lon"), P(), P("mem"), P("lat"), P(), P(), P(), P()),
        out_specs=(P("mem", None, "lat", "lon"), P(None, "lat", "lon")),
        check_vma=False,
    )
```

profile of v0, /device:TPU:2, one launch (start us, length us, event | category | flops | bytes accessed | tf_op | source)
XLA Modules:
  0.0 758.4 jit_solution(7995749304331995080)
XLA Ops:
  8.7 405.1 %all-gather.2.cloned.1.call-done = bf16[256,73,8,128]{3,2,1,0:T(8,128)(2,1)} async-done(((bf16[16,73,8,128]{3,2,1,0:T(8,128)(2,1)}), bf16[256,73,8,128]{3,2,1,0:T(8,128)(2,1)}) %all-gather.2.cloned.1.call-update) | async-done | bytes 38273040 | tf_op jit(solution)/shard_map/all_gather | solution.py:75
  413.9 3.8 gather_fusion
  420.6 3.4 collective-permute-start
  424.7 2.5 collective-permute-start.1
  427.2 36.3 %while.24 = (s32[]{:T(128)}, f32[73,8,128]{2,1,0:T(8,128)S(1)}, f32[16]{0:T(128)S(1)}, bf16[16,73,8,128]{3,2,1,0:T(8,128)(2,1)}) while((s32[]{:T(128)}, f32[73,8,128]{2,1,0:T(8,128)S(1)}, f32[16]{0:T(128)S(1)}, bf16[16,73,8,128]{3,2,1,0:T(8,128)(2,1)}) %tuple.76), condition=%wide.region_4.5_spmd.clone.clone, body=%wide.region_3.4_spmd.clone.sunk.clone | while | flops 299011 | bytes 747603 | solution.py:114
  464.3 32.7 %psum.15 = f32[]{:T(128)} all-reduce(f32[]{:T(128)} %reduce_sum.18), channel_id=1, replica_groups=mesh['mem'=16,'lat'=4,'lon'=4] {'mem'}, use_global_device_ids=true, to_apply=%region_7.8 | all-reduce | flops 1 | bytes 8 | tf_op jit(solution)/shard_map/psum | solution.py:115
  500.1 3.3 pad_maximum_fusion.1
  503.4 5.8 fusion.29
  509.2 5.2 copy.45
  514.5 5.1 copy.46
  519.6 3.5 collective-permute-start.3
  523.1 72.4 %all-reduce.2.cloned.1.call-done = f32[73,8,128]{2,1,0:T(8,128)} async-done(((f32[73,8,128]{2,1,0:T(8,128)}), f32[73,8,128]{2,1,0:T(8,128)}) %all-reduce.2.cloned.1.call-update) | async-done | bytes 299024 | tf_op jit(solution)/shard_map/psum | solution.py:115
  597.8 4.3 copy.47
  602.1 4.3 copy.48
  606.3 16.0 %pad_maximum_fusion = bf16[16,73,10,130]{3,2,1,0:T(8,128)(2,1)} fusion(bf16[16,73,10,1]{3,2,1,0:T(8,128)(2,1)} %copy.48, bf16[16,73,1,128]{3,2,1,0:T(2,128)(2,1)} %copy-done.1, bf16[16,73,8,128]{3,2,1,0:T(8,128)(2,1)S(1)} %select_select_fusion, bf16[16,73,1,128]{3,2,1,0:T(2,128)(2,1)S(1)} %copy.43, bf16[16,73,10,1]{3,2,1,0:T(8,128)(2,1)} %copy.47), kind=kLoop, calls=%fused_computation.51 | loop fusion | flops 15184000 | bytes 6073600 | tf_op jit(solution)/shard_map/concatenate | solution.py:20
  622.3 129.2 %while.23 = (s32[]{:T(128)}, bf16[16,73,8,128]{3,2,1,0:T(8,128)(2,1)}, f32[9,73,8]{1,2,0:T(8,128)S(1)}, bf16[16,73,10,130]{3,2,1,0:T(8,128)(2,1)}, f32[73]{0:T(1...) while((s32[]{:T(128)}, ...), condition=%wide.region_2.3_spmd.clone, body=%wide.region_0.2_spmd.sunk.clone | while | flops 475396800 | bytes 8175199 | solution.py:68
  626.2 3.5 fusion.45
  634.2 3.5 fusion.45
  642.3 3.5 fusion.45
  650.4 3.5 fusion.45
  658.5 3.5 fusion.45
  666.5 3.5 fusion.45
  674.6 3.5 fusion.45
  682.7 3.5 fusion.45
  690.8 3.5 fusion.45
  698.8 3.5 fusion.45
  706.9 3.5 fusion.45
  715.0 3.5 fusion.45
  723.1 3.5 fusion.45
  731.1 3.5 fusion.45
  739.2 3.5 fusion.45
  747.3 3.5 fusion.45
  (407 shorter events, 119.2 us)
Async XLA Ops:
  7.2 406.7 %all-gather.2.cloned.1.call-start = ((), (), s32[]{:S(2)}) async-start(), calls=%async_computation | async-start | bytes 40665088 | tf_op jit(solution)/shard_map/all_gather | solution.py:75
  7.9 587.6 %all-reduce.2.cloned.1.call-start = ((), (), s32[]{:S(2)}) async-start(), calls=%async_computation.1 | async-start | bytes 598016 | tf_op jit(solution)/shard_map/psum | solution.py:115
  417.7 9.5 %copy-start.6 = (f32[16]{0:T(128)S(1)}, f32[16]{0:T(128)}, u32[]{:S(2)}) copy-start(f32[16]{0:T(128)} %param.14) | copy-start | bytes 196
  419.7 77.2 %copy-start.2 = (f32[8,9,73]{2,0,1:T(8,128)S(1)}, f32[8,9,73]{2,0,1:T(8,128)}, u32[]{:S(2)}) copy-start(f32[8,9,73]{2,0,1:T(8,128)} %param.16) | copy-start | bytes 63076
  419.7 77.4 %copy-start.4 = (s32[8]{0:T(128)S(1)}, s32[8]{0:T(128)}, u32[]{:S(2)}) copy-start(s32[8]{0:T(128)} %param.15) | copy-start | bytes 100
  420.6 76.8 %collective-permute-start = (bf16[16,73,1,128]{3,0,2,1:T(8,128)(2,1)S(1)}, bf16[16,73,1,128]{3,0,2,1:T(8,128)(2,1)S(1)}, u32[]{:S(2)}, u32[]{:S(2)}) collective-permute-start(bf16[16,73,1,128]{3,0,2,1:T(8,128)(2,1)S(1)} %copy.41), channel_id=1, source_target_pairs={{0,4},{4,8},{8,12},{1,5},{5,9},{9,13},{2,6},{6,10},{10,14},{3,7},{... | collective-permute-start | bytes 897032 | tf_op jit(solution)/shard_map/ppermute | solution.py:16
  424.7 73.1 %collective-permute-start.1 = (bf16[16,73,1,128]{3,0,2,1:T(8,128)(2,1)}, bf16[16,73,1,128]{3,0,2,1:T(8,128)(2,1)}, u32[]{:S(2)}, u32[]{:S(2)}) collective-permute-start(bf16[16,73,1,128]{3,0,2,1:T(8,128)(2,1)} %copy.42), channel_id=1, source_target_pairs={{4,0},{8,4},{12,8},{5,1},{9,5},{13,9},{6,2},{10,6},{14,10},{7,3},{... | collective-permute-start | bytes 897032 | tf_op jit(solution)/shard_map/ppermute | solution.py:19
  463.6 0.7 copy-start
  499.3 0.8 copy-start.1
  514.4 83.4 %collective-permute-start.2 = (bf16[16,73,10,1]{1,0,3,2:T(8,128)(2,1)S(1)}, bf16[16,73,10,1]{1,0,3,2:T(8,128)(2,1)S(1)}, u32[]{:S(2)}, u32[]{:S(2)}) collective-permute-start(bf16[16,73,10,1]{1,0,3,2:T(8,128)(2,1)S(1)} %copy.45), channel_id=1, source_target_pairs={{0,1},{1,2},{2,3},{3,0},{4,5},{5,6},{6,7},{7,4},{8,9},{9,10},{10,1... | collective-permute-start | bytes 70088 | tf_op jit(solution)/shard_map/ppermute | solution.py:16
  519.6 82.4 %collective-permute-start.3 = (bf16[16,73,10,1]{1,0,3,2:T(8,128)(2,1)S(1)}, bf16[16,73,10,1]{1,0,3,2:T(8,128)(2,1)S(1)}, u32[]{:S(2)}, u32[]{:S(2)}) collective-permute-start(bf16[16,73,10,1]{1,0,3,2:T(8,128)(2,1)S(1)} %copy.46), channel_id=1, source_target_pairs={{1,0},{2,1},{3,2},{0,3},{5,4},{6,5},{7,6},{4,7},{9,8},{10,9},{11,1... | collective-permute-start | bytes 70088 | tf_op jit(solution)/shard_map/ppermute | solution.py:19
  606.3 16.0 %copy-start.3 = (f32[73]{0:T(128)S(1)}, f32[73]{0:T(128)}, u32[]{:S(2)}) copy-start(f32[73]{0:T(128)} %param.17) | copy-start | bytes 880
  606.3 16.0 %copy-start.5 = (bf16[1536,73]{0,1:T(8,128)(2,1)S(1)}, bf16[1536,73]{0,1:T(8,128)(2,1)}, u32[]{:S(2)}) copy-start(bf16[1536,73]{0,1:T(8,128)(2,1)} %param.18) | copy-start | bytes 672772
Sparse Core Ops, SparseCore 0:
  9.8 404.0 all-gather.1
  464.4 131.0 all-reduce.1
where the time goes:
time: 760 us; the launch traced here: 758 us
  waiting for transfers between devices  478 us (63%)
  other arithmetic  95.7 us (13%)
  local copies, waits for them, and re-layouts  70.1 us (9%)
  matrix products  56.3 us (7%)
  blocking collectives  32.7 us (4%)
  between operations  14.2 us (2%)
  starting transfers between devices  9.5 us (1%)
    all_gather x1, waiting for transfers between devices, replicate_tiles(): shard_rows = lax.all_gather(member_tiles, 'mem', axis=0, tiled=True)  405 us
    psum x1, waiting for transfers between devices, shards(): lax.psum((weighted_part, jnp.sum(obs_weights)), 'mem')  72.4 us
    dot_general x16, matrix products, finish(): jnp.dot(exit_projection_matrix, hidden, preferred_element_type=jnp.float32)  56.1 us
    psum x1, blocking collectives, shards(): lax.psum((weighted_part, jnp.sum(obs_weights)), 'mem')  32.7 us
    add x16, other arithmetic, accumulate(): return (total + weight * particle_state.astype(jnp.float32), None)  26.6 us
    reduce_sum x16, other arithmetic, finish(): mean_sq = jnp.mean(conv * conv, axis=0)  21.8 us
    convert_element_type x16, other arithmetic, one_member(): padded = padded_tile.astype(jnp.float32)  19.4 us
    concatenate x2, other arithmetic, extended(): block = jnp.concatenate([low, block, high], axis=dim)  19.3 us
  transfers between devices with their start and end apart: 6, of which 2 were waited for; matrix products, arithmetic and copies ran while one was open for 9% of the time, Pallas kernels for 0%

commit v1 on v0

--- a/solution.py
+++ b/solution.py
@@ -72,7 +72,9 @@
     my_index = lax.axis_index("mem")
     per_device = member_tiles.shape[0]
     own_parents = lax.dynamic_slice_in_dim(ancestry, my_index * per_device, per_device)
-    shard_rows = lax.all_gather(member_tiles, "mem", axis=0, tiled=True)
+    shard_rows = jnp.concatenate(
+        lax.all_to_all(jnp.stack([member_tiles] * lax.axis_size("mem")), "mem", 0, 0), axis=0
+    )
     row_total = shard_rows.shape[0]
     inside = (own_parents >= 0) & (own_parents < row_total)
     picked = jnp.take(shard_rows, jnp.clip(own_parents, 0, row_total - 1), axis=0)

time: 760 us -> 1290 us (1.70)
  waiting for transfers between devices: 478 us -> 937 us
  blocking collectives: 32.7 us -> 76.2 us
  local copies, waits for them, and re-layouts: 70.1 us -> 84.1 us
    all_to_all x0 -> x1, waiting for transfers between devices: none -> 863 us  [replicate_tiles(): lax.all_to_all(jnp.stack([member_tiles] * lax.axis_size('mem')), 'mem', 0...]
    all_gather x1 -> x0, waiting for transfers between devices: 405 us -> none  [replicate_tiles(): shard_rows = lax.all_gather(member_tiles, 'mem', axis=0, tiled=True)]
    psum x1, blocking collectives: 32.7 us -> 76.2 us  [shards(): lax.psum((weighted_part, jnp.sum(obs_weights)), 'mem')]
    another operation x0 -> x1, local copies, waits for them, and re-layouts: none -> 14 us  [replicate_tiles(): jnp.stack([member_tiles] * lax.axis_size('mem'))]
  transfers between devices with their start and end apart: 6 -> 6, of which waited for: 2 -> 2; matrix products, arithmetic and copies ran while one was open for 9% -> 5% of each run, Pallas kernels for 0% -> 0%
where the time goes in v1:
time: 1290 us; the launch traced here: 1280 us
  waiting for transfers between devices  937 us (73%)
  other arithmetic  95 us (7%)
  local copies, waits for them, and re-layouts  84.1 us (7%)
  blocking collectives  76.2 us (6%)
  matrix products  56.2 us (4%)
  starting transfers between devices  19.2 us (1%)
  between operations  14.2 us (1%)
    all_to_all x1, waiting for transfers between devices, replicate_tiles(): lax.all_to_all(jnp.stack([member_tiles] * lax.axis_size('mem')), 'mem', 0...  863 us
    psum x1, blocking collectives, shards(): lax.psum((weighted_part, jnp.sum(obs_weights)), 'mem')  76.2 us
    psum x1, waiting for transfers between devices, shards(): lax.psum((weighted_part, jnp.sum(obs_weights)), 'mem')  74.2 us
    dot_general x16, matrix products, finish(): jnp.dot(exit_projection_matrix, hidden, preferred_element_type=jnp.float32)  55.9 us
    add x16, other arithmetic, accumulate(): return (total + weight * particle_state.astype(jnp.float32), None)  26.6 us
  transfers between devices with their start and end apart: 6, of which 2 were waited for; matrix products, arithmetic and copies ran while one was open for 5% of the time, Pallas kernels for 0%

profile of v1, /device:TPU:2, one launch (start us, length us, event | category | flops | bytes accessed | tf_op | source)
XLA Modules:
  0.0 1283.8 jit_solution(3802628760393443240)
XLA Ops:
  7.2 14.0 %stack.2 = bf16[16,16,73,8,128]{4,3,2,1,0:T(8,128)(2,1)} broadcast(bf16[16,73,8,128]{3,2,1,0:T(8,128)(2,1)} %param.12), dimensions={1,2,3,4} | broadcast | bytes 40665088 | tf_op jit(solution)/shard_map/stack | solution.py:76
  21.1 9.8 all-to-all-start
  31.1 863.2 %all-to-all-done = bf16[16,16,73,8,128]{4,3,2,1,0:T(8,128)(2,1)} async-done(((bf16[16,16,73,8,128]{4,3,2,1,0:T(8,128)(2,1)}), bf16[16,16,73,8,128]{4,3,2,1,0:T(8,128)(2,1)}, u32[]{:S(2)}, u32[]{:S(2)}) %all-to-all-start) | async-done | bytes 38273056 | tf_op jit(solution)/shard_map/all_to_all | solution.py:76
  894.2 3.8 gather_fusion
  900.9 3.4 collective-permute-start
  907.6 36.3 %while.24 = (s32[]{:T(128)}, f32[73,8,128]{2,1,0:T(8,128)S(1)}, f32[16]{0:T(128)S(1)}, bf16[16,73,8,128]{3,2,1,0:T(8,128)(2,1)}) while((s32[]{:T(128)}, f32[73,8,128]{2,1,0:T(8,128)S(1)}, f32[16]{0:T(128)S(1)}, bf16[16,73,8,128]{3,2,1,0:T(8,128)(2,1)}) %tuple.75), condition=%wide.region_4.5_spmd.clone.clone, body=%wide.region_3.4_spmd.clone.sunk.clone | while | flops 299011 | bytes 747603 | solution.py:116
  944.6 76.2 %psum.15 = f32[]{:T(128)} all-reduce(f32[]{:T(128)} %reduce_sum.18), channel_id=1, replica_groups=mesh['mem'=16,'lat'=4,'lon'=4] {'mem'}, use_global_device_ids=true, to_apply=%region_7.8 | all-reduce | flops 1 | bytes 8 | tf_op jit(solution)/shard_map/psum | solution.py:117
  1027.2 5.8 fusion.29
  1033.0 5.1 copy.63
  1038.3 5.2 copy.64
  1043.5 3.5 collective-permute-start.3
  1046.9 74.2 %all-reduce.2.cloned.1.call-done = f32[73,8,128]{2,1,0:T(8,128)} async-done(((f32[73,8,128]{2,1,0:T(8,128)}), f32[73,8,128]{2,1,0:T(8,128)}) %all-reduce.2.cloned.1.call-update) | async-done | bytes 299024 | tf_op jit(solution)/shard_map/psum | solution.py:117
  1123.4 4.3 copy.65
  1127.6 4.3 copy.66
  1131.9 16.0 %pad_maximum_fusion = bf16[16,73,10,130]{3,2,1,0:T(8,128)(2,1)} fusion(bf16[16,73,10,1]{3,2,1,0:T(8,128)(2,1)} %copy.66, bf16[16,73,1,128]{3,2,1,0:T(2,128)(2,1)} %copy-done.1, bf16[16,73,8,128]{3,2,1,0:T(8,128)(2,1)S(1)} %select_select_fusion, bf16[16,73,1,128]{3,2,1,0:T(2,128)(2,1)S(1)} %copy.61, bf16[16,73,10,1]{3,2,1,0:T(8,128)(2,1)} %copy.65), kind=kLoop, calls=%fused_computation.51 | loop fusion | flops 15184000 | bytes 6073600 | tf_op jit(solution)/shard_map/concatenate | solution.py:20
  1147.9 129.1 %while.23 = (s32[]{:T(128)}, bf16[16,73,8,128]{3,2,1,0:T(8,128)(2,1)}, f32[9,73,8]{1,2,0:T(8,128)S(1)}, bf16[16,73,10,130]{3,2,1,0:T(8,128)(2,1)}, f32[73]{0:T(1...) while((s32[]{:T(128)}, ...), condition=%wide.region_2.3_spmd.clone, body=%wide.region_0.2_spmd.sunk.clone | while | flops 475396800 | bytes 8175199 | solution.py:68
  1151.7 3.5 fusion.45
  1159.8 3.5 fusion.45
  1167.9 3.5 fusion.45
  1176.0 3.5 fusion.45
  1184.0 3.5 fusion.45
  1192.1 3.5 fusion.45
  1200.2 3.5 fusion.45
  1208.2 3.5 fusion.45
  1216.3 3.5 fusion.45
  1224.4 3.5 fusion.45
  1232.4 3.5 fusion.45
  1240.5 3.5 fusion.45
  1248.6 3.5 fusion.45
  1256.6 3.5 fusion.45
  1264.7 3.5 fusion.45
  1272.8 3.5 fusion.45
  (409 shorter events, 123.6 us)
Async XLA Ops:
  21.1 9.8 copy-start.5
  21.1 873.1 %all-to-all-start = ((bf16[16,16,73,8,128]{4,3,2,1,0:T(8,128)(2,1)}), bf16[16,16,73,8,128]{4,3,2,1,0:T(8,128)(2,1)}, u32[]{:S(2)}, u32[]{:S(2)}) async-start(bf16[16,16,73,8,128]{4,3,2,1,0:T(8,128)(2,1)} %stack.2), calls=%async_computation | async-start | bytes 76546048 | tf_op jit(solution)/shard_map/all_to_all | solution.py:76
  30.9 1090.2 %all-reduce.2.cloned.1.call-start = ((), (), s32[]{:S(2)}) async-start(), calls=%async_computation.1 | async-start | bytes 598016 | tf_op jit(solution)/shard_map/psum | solution.py:117
  898.0 9.5 copy-start.7
  900.1 120.7 %copy-start.2 = (f32[8,9,73]{2,0,1:T(8,128)S(1)}, f32[8,9,73]{2,0,1:T(8,128)}, u32[]{:S(2)}) copy-start(f32[8,9,73]{2,0,1:T(8,128)} %param.16) | copy-start | bytes 63076
  900.1 120.9 %copy-start.4 = (s32[8]{0:T(128)S(1)}, s32[8]{0:T(128)}, u32[]{:S(2)}) copy-start(s32[8]{0:T(128)} %param.15) | copy-start | bytes 100
  900.9 120.3 %collective-permute-start = (bf16[16,73,1,128]{3,0,2,1:T(8,128)(2,1)S(1)}, bf16[16,73,1,128]{3,0,2,1:T(8,128)(2,1)S(1)}, u32[]{:S(2)}, u32[]{:S(2)}) collective-permute-start(bf16[16,73,1,128]{3,0,2,1:T(8,128)(2,1)S(1)} %copy.59), channel_id=1, source_target_pairs={{0,4},{4,8},{8,12},{1,5},{5,9},{9,13},{2,6},{6,10},{10,14},{3,7},{... | collective-permute-start | bytes 897032 | tf_op jit(solution)/shard_map/ppermute | solution.py:16
  905.1 116.6 %collective-permute-start.1 = (bf16[16,73,1,128]{3,0,2,1:T(8,128)(2,1)}, bf16[16,73,1,128]{3,0,2,1:T(8,128)(2,1)}, u32[]{:S(2)}, u32[]{:S(2)}) collective-permute-start(bf16[16,73,1,128]{3,0,2,1:T(8,128)(2,1)} %copy.60), channel_id=1, source_target_pairs={{4,0},{8,4},{12,8},{5,1},{9,5},{13,9},{6,2},{10,6},{14,10},{7,3},{... | collective-permute-start | bytes 897032 | tf_op jit(solution)/shard_map/ppermute | solution.py:19
  943.9 0.7 copy-start
  1023.1 0.8 copy-start.1
  1038.2 85.2 %collective-permute-start.2 = (bf16[16,73,10,1]{1,0,3,2:T(8,128)(2,1)S(1)}, bf16[16,73,10,1]{1,0,3,2:T(8,128)(2,1)S(1)}, u32[]{:S(2)}, u32[]{:S(2)}) collective-permute-start(bf16[16,73,10,1]{1,0,3,2:T(8,128)(2,1)S(1)} %copy.63), channel_id=1, source_target_pairs={{0,1},{1,2},{2,3},{3,0},{4,5},{5,6},{6,7},{7,4},{8,9},{9,10},{10,1... | collective-permute-start | bytes 70088 | tf_op jit(solution)/shard_map/ppermute | solution.py:16
  1043.5 84.2 %collective-permute-start.3 = (bf16[16,73,10,1]{1,0,3,2:T(8,128)(2,1)S(1)}, bf16[16,73,10,1]{1,0,3,2:T(8,128)(2,1)S(1)}, u32[]{:S(2)}, u32[]{:S(2)}) collective-permute-start(bf16[16,73,10,1]{1,0,3,2:T(8,128)(2,1)S(1)} %copy.64), channel_id=1, source_target_pairs={{1,0},{2,1},{3,2},{0,3},{5,4},{6,5},{7,6},{4,7},{9,8},{10,9},{11,1... | collective-permute-start | bytes 70088 | tf_op jit(solution)/shard_map/ppermute | solution.py:19
  1131.9 16.0 %copy-start.3 = (f32[73]{0:T(128)S(1)}, f32[73]{0:T(128)}, u32[]{:S(2)}) copy-start(f32[73]{0:T(128)} %param.17) | copy-start | bytes 880
  1131.9 16.0 %copy-start.6 = (bf16[1536,73]{0,1:T(8,128)(2,1)S(1)}, bf16[1536,73]{0,1:T(8,128)(2,1)}, u32[]{:S(2)}) copy-start(bf16[1536,73]{0,1:T(8,128)(2,1)} %param.18) | copy-start | bytes 672772
Sparse Core Ops, SparseCore 0:
  944.8 176.3 all-reduce.1
